TPU v7x, 32 devices: a whole 2x2x4 slice. The times are simulated.
32 devices in a mesh: dp: 16 (over z, y, core), own: 2 (over x).
Axes of the slice: x: 2, y: 2, z: 4, core: 2. Of those that a mesh axis runs over, the one named last changes fastest.
Arguments:
- layer_inputs: bfloat16 [4, 16, 16, 128, 128], P(None, 'dp', 'own'), as said below
- weights: bfloat16 [4, 1152, 128], replicated, may hold values from -0.1875 to 0.1875
- top_cotangent: bfloat16 [16, 16, 128, 128], P('dp', 'own'), may hold values from -6 to 6
- segmentation: int32 [16, 16, 128], P('dp', 'own'), may hold values from 0 to 2
- layer_slots: int32 [4], replicated, may hold values from 0 to 3, as said below
- a_inverse: bfloat16 [4, 1152, 1152], P('own', 'dp'), as said below
- g_inverse: bfloat16 [4, 128, 128], P('own'), as said below
Outputs:
- preconditioned: float32 [4, 1152, 128], P(None, 'dp')
- input_grad: bfloat16 [16, 16, 128, 128], P('dp', 'own')
Inputs may be any that keep to these rules, and one draw needn't show every extreme that they name: Distinct slot numbers; layer l is held by owner layer_slots[l] // 2, in that owner's slot layer_slots[l] % 2. One owner holds exactly 2 layers in every draw. `a_inverse`: each factor is symmetric. `g_inverse`: each factor is symmetric. `layer_inputs`: activations after a rectifier.
All inputs are finite; a program needn't handle non-finite values.
Results may differ from a plain program's by a relative error of at most 0.011.
Values may be sent and summed in bfloat16 or wider, within the bound.
A program may use at most 64 MiB of HBM per device.

v0:
```python
import math
import jax
import jax.numpy as jnp
from jax import lax
from jax.sharding import PartitionSpec as P


def extended(cells, sides, width):
    for axis, dim in sides:
        count = lax.axis_size(axis)
        ends = count - 1
        head = lax.slice_in_dim(cells, 0, width, axis=dim)
        tail = lax.slice_in_dim(cells, cells.shape[dim] - width, cells.shape[dim], axis=dim)
        cells = jnp.concatenate(
            [
                lax.ppermute(tail, axis, [(i, (i + 1) % count) for i in range(ends)]),
                cells,
                lax.ppermute(head, axis, [((i + 1) % count, i) for i in range(ends)]),
            ],
            axis=dim,
        )
    return cells


def from_root(block, axis, owner):
    block = jnp.where(lax.axis_index(axis) == owner, block, jnp.zeros_like(block))
    return lax.psum(block, axis)


def loss_weight(labels):
    return jnp.where(labels == 0, 1.0, jnp.where(labels == 1, 0.0, 0.5)).astype(jnp.float32)


def tap_matrix(padded, num_rows, num_cols):
    channels = padded.shape[-1]
    pieces = []
    for tap_index in range(9):
        row_start = 2 - tap_index // 3
        col_start = 2 - tap_index % 3
        pieces.append(padded[row_start : row_start + num_rows, col_start : col_start + num_cols])
    stacked = jnp.stack(pieces, axis=2)
    return stacked.reshape(num_rows * num_cols, 9 * channels)


def per_device(
    layer_inputs, weights, top_cotangent, segmentation, layer_slots, a_inverse, g_inverse
):
    layer_count = layer_inputs.shape[0]
    num_rows = layer_inputs.shape[2]
    num_cols = layer_inputs.shape[3]
    channels = layer_inputs.shape[4]
    data_devices = lax.axis_size("dp")
    owner_devices = lax.axis_size("own")
    grad_scale = 1.0 / math.sqrt(data_devices * owner_devices * num_rows * num_cols)
    inputs_local = layer_inputs[:, 0]
    scaled = loss_weight(segmentation[0])[:, :, None] * top_cotangent[0].astype(jnp.float32)
    out_grad = scaled.astype(jnp.bfloat16)
    grad_blocks = [None] * layer_count
    input_grad = None
    for layer_index in range(layer_count - 1, -1, -1):
        rimmed = extended(out_grad, (("own", 0),), 1)
        padded = jnp.pad(rimmed, ((0, 0), (1, 1), (0, 0)))
        tap_rows = tap_matrix(padded, num_rows, num_cols)
        flat_inputs = inputs_local[layer_index].reshape(num_rows * num_cols, channels)
        grad_block = lax.dot_general(
            flat_inputs, tap_rows, (((0,), (0,)), ((), ())), preferred_element_type=jnp.float32
        )
        grad_blocks[layer_index] = grad_block.reshape(9 * channels, channels) * grad_scale
        kernel = weights[layer_index].reshape(channels, 9 * channels)
        input_side = lax.dot_general(
            tap_rows, kernel, (((1,), (1,)), ((), ())), preferred_element_type=jnp.float32
        )
        input_side = input_side.reshape(num_rows, num_cols, channels)
        if layer_index > 0:
            out_grad = jnp.where(inputs_local[layer_index] > 0, input_side, 0.0).astype(
                jnp.bfloat16
            )
        else:
            input_grad = input_side.astype(jnp.bfloat16)[None]
    grad_term = jnp.concatenate(grad_blocks, axis=1)
    grad_rows = lax.psum_scatter(grad_term, "dp", scatter_dimension=0, tiled=True)
    slot_count = a_inverse.shape[0]
    grad_sum = lax.psum(grad_rows.astype(jnp.bfloat16), "own")
    left_panels = []
    right_panels = []
    for layer_index in range(layer_count):
        slot_id = layer_slots[layer_index]
        owner_index = slot_id // slot_count
        local_slot = slot_id % slot_count
        left_panel = lax.dynamic_index_in_dim(a_inverse, local_slot, 0, keepdims=False)
        right_panel = lax.dynamic_index_in_dim(g_inverse, local_slot, 0, keepdims=False)
        left_panel, right_panel = (
            from_root(left_panel, "own", owner_index),
            from_root(right_panel, "own", owner_index),
        )
        left_panels.append(left_panel)
        right_panels.append(right_panel)
    left_stack = jnp.stack(left_panels, axis=0)
    right_stack = jnp.stack(right_panels, axis=0)
    gathered_piece = lax.all_gather(grad_sum, "dp", axis=0, tiled=True)
    width_here = gathered_piece.shape[0]
    shaped_piece = gathered_piece.reshape(width_here, layer_count, channels)
    left_product = jnp.einsum(
        "lrn,nlc->lrc", left_stack, shaped_piece, preferred_element_type=jnp.float32
    )
    preconditioned = jnp.einsum(
        "lrc,lcd->lrd",
        left_product.astype(jnp.bfloat16),
        right_stack,
        preferred_element_type=jnp.float32,
    )
    return (preconditioned, input_grad)


def solution(mesh):
    in_specs = (
        P(None, "dp", "own", None, None),
        P(),
        P("dp", "own", None, None),
        P("dp", "own", None),
        P(),
        P("own", "dp", None),
        P("own", None, None),
    )
    out_specs = (P(None, "dp", None), P("dp", "own", None, None))
    return jax.shard_map(
        per_device, mesh=mesh, in_specs=in_specs, out_specs=out_specs, check_vma=False
    )
```

profile of v0, /device:TPU:0, one launch (start us, length us, event | category | flops | bytes accessed | tf_op | source)
XLA Modules:
  0.0 266.4 jit_solution(8736624988374941266)
XLA Ops:
  9.2 1.3 collective-permute-start.1
  10.5 4.8 %collective-permute-start = (bf16[1,128,128]{1,2,0:T(8,128)(2,1)S(1)}, bf16[1,128,128]{1,2,0:T(8,128)(2,1)S(1)}, u32[]{:S(2)}, u32[]{:S(2)}) collective-permute-start(bf16[1,128,128]{1,2,0:T(8,128)(2,1)S(1)} %get-tuple-element.29), channel_id=1, source_target_pairs={{0,1},{2,3},{4,5},{6,7},{8,9},{10,11},{12,13},{14,15},{16,17},{18,... | collective-permute-start | bytes 98312 | tf_op jit(solution)/shard_map/ppermute | solution.py:16
  15.4 1.3 fusion.111
  21.5 1.6 copy.30
  23.1 1.8 fusion.13
  26.9 5.1 %collective-permute-start.2 = (bf16[1,128,128]{2,1,0:T(8,128)(2,1)}, bf16[1,128,128]{2,1,0:T(8,128)(2,1)S(1)}, u32[]{:S(2)}, u32[]{:S(2)}) collective-permute-start(bf16[1,128,128]{2,1,0:T(8,128)(2,1)} %get-tuple-element.27), channel_id=1, source_target_pairs={{0,1},{2,3},{4,5},{6,7},{8,9},{10,11},{12,13},{14,15},{16,17},{18,... | collective-permute-start | bytes 98312 | tf_op jit(solution)/shard_map/ppermute | solution.py:16
  36.1 2.7 copy.28
  38.8 2.5 copy.20
  41.2 2.7 %fusion.14 = bf16[8,128,128]{2,1,0:T(8,128)(2,1)S(1)} fusion(bf16[8,128,1152]{1,2,0:T(8,128)(2,1)} %bitcast.255, bf16[128,1152,1]{1,0,2:T(8,128)(2,1)} %reshape.135, bf16[4,1,8,128,128]{4,3,2,1,0:T(8,128)(2,1)} %param.7), kind=kOutput, calls=%fused_computation.24 | convolution fusion | flops 302383104 | bytes 3178496 | tf_op jit(solution)/shard_map/dot_general | solution.py:70
  44.6 1.3 collective-permute-start.5
  45.9 5.3 %collective-permute-start.4 = (bf16[1,128,128]{2,1,0:T(8,128)(2,1)}, bf16[1,128,128]{2,1,0:T(8,128)(2,1)S(1)}, u32[]{:S(2)}, u32[]{:S(2)}) collective-permute-start(bf16[1,128,128]{2,1,0:T(8,128)(2,1)} %get-tuple-element.25), channel_id=1, source_target_pairs={{0,1},{2,3},{4,5},{6,7},{8,9},{10,11},{12,13},{14,15},{16,17},{18,... | collective-permute-start | bytes 98312 | tf_op jit(solution)/shard_map/ppermute | solution.py:16
  51.2 1.6 fusion.2
  52.8 1.3 copy.29
  57.2 2.7 copy.26
  59.9 2.5 copy.22
  62.3 2.7 %fusion.15 = bf16[8,128,128]{2,1,0:T(8,128)(2,1)S(1)} fusion(bf16[8,128,1152]{1,2,0:T(8,128)(2,1)} %bitcast.256, bf16[128,1152,1]{1,0,2:T(8,128)(2,1)} %reshape.136, bf16[4,1,8,128,128]{4,3,2,1,0:T(8,128)(2,1)} %param.7), kind=kOutput, calls=%fused_computation.25 | convolution fusion | flops 302383104 | bytes 3178496 | tf_op jit(solution)/shard_map/dot_general | solution.py:70
  67.0 5.1 %collective-permute-start.6 = (bf16[1,128,128]{2,1,0:T(8,128)(2,1)}, bf16[1,128,128]{2,1,0:T(8,128)(2,1)S(1)}, u32[]{:S(2)}, u32[]{:S(2)}) collective-permute-start(bf16[1,128,128]{2,1,0:T(8,128)(2,1)} %get-tuple-element.23), channel_id=1, source_target_pairs={{0,1},{2,3},{4,5},{6,7},{8,9},{10,11},{12,13},{14,15},{16,17},{18,... | collective-permute-start | bytes 98312 | tf_op jit(solution)/shard_map/ppermute | solution.py:16
  72.2 1.6 fusion.1
  73.7 1.3 copy.27
  78.1 2.7 copy.24
  80.8 3.3 %fusion = f32[128,1152]{0,1:T(8,128)} fusion(bf16[1024,128]{1,0:T(8,128)(2,1)S(1)} %bitcast.258, bf16[144,8,8,128]{3,2,1,0:T(8,128)(2,1)} %bitcast.257), kind=kOutput, calls=%fused_computation.4 | convolution fusion | flops 302137344 | bytes 3211264 | tf_op jit(solution)/shard_map/dot_general | solution.py:65
  84.0 2.1 copy.25
  86.2 1.9 mul.59
  88.1 3.0 %pad_maximum_fusion = f32[1152,512]{1,0:T(8,128)} fusion(f32[1152,128]{1,0:T(8,128)S(1)} %mul.68, f32[1152,128]{1,0:T(8,128)} %mul.65, f32[1152,128]{1,0:T(8,128)} %mul.62, f32[1152,128]{1,0:T(8,128)} %mul.59), kind=kLoop, calls=%fused_computation.16 | loop fusion | flops 1769472 | bytes 4718592 | tf_op jit(solution)/shard_map/concatenate | solution.py:80
  103.5 52.2 %reduce-scatter.2.cloned.1.call-done = f32[72,512]{1,0:T(8,128)} async-done(((f32[1152,512]{1,0:T(8,128)}), f32[72,512]{1,0:T(8,128)}) %reduce-scatter.2.cloned.1.call-update) | async-done | bytes 147472 | tf_op jit(solution)/shard_map/reduce_scatter | solution.py:81
  155.7 1.6 convert_element_type.58
  158.1 34.0 %all-reduce.11.cloned.1.call-done = (bf16[72,512]{1,0:T(8,128)(2,1)}, bf16[1,72,1152]{2,1,0:T(8,128)(2,1)}, bf16[1,72,1152]{2,1,0:T(8,128)(2,1)}, bf16[1,72,1152]{2,1,0:T(8,128)(2,1)}, bf16[1,72,1152]{2,1,0:T(8,128)(2,1)}) async-done(((bf16[72,512]{1,0:T(8,128)(2,1)}, bf16[1,72,1152]{2,1,0:T(8,128)(2,1)}, bf16[1,72,1152]{2,1,0:T(8,128)(2,1)}, bf16[1,72,1152]{2,1,0:T(8,128)(2,1)}, ...) | async-done | bytes 737296 | tf_op jit(solution)/shard_map/psum | solution.py:83
  192.4 2.5 copy.32
  194.9 3.3 %fusion.19 = bf16[1,8,128,128]{3,2,1,0:T(8,128)(2,1)} fusion(bf16[8,128,1152]{1,2,0:T(8,128)(2,1)} %bitcast.250, bf16[128,1152,1]{1,0,2:T(8,128)(2,1)S(1)} %reshape.137), kind=kOutput, calls=%fused_computation.30 | convolution fusion | flops 302120960 | bytes 2916352 | tf_op jit(solution)/shard_map/dot_general | solution.py:70
  198.2 18.3 %all-reduce.9.cloned.1.call-done = (bf16[1,128,128]{2,1,0:T(8,128)(2,1)}, bf16[1,128,128]{2,1,0:T(8,128)(2,1)}, bf16[1,128,128]{2,1,0:T(8,128)(2,1)}, bf16[1,128,128]{2,1,0:T(8,128)(2,1)}) async-done(((bf16[1,128,128]{2,1,0:T(8,128)(2,1)}, bf16[1,128,128]{2,1,0:T(8,128)(2,1)}, bf16[1,128,128]{2,1,0:T(8,128)(2,1)}, bf16[1,128,128]{2,1,0:T(8,128)(2,1)}), (bf16[1,128,128]{2,1,0:T(8,128)(2,1)}, ...) | async-done | bytes 131088 | tf_op jit(solution)/shard_map/psum | solution.py:27
  216.5 40.8 %all-gather.2.cloned.1.call-done = bf16[1152,512]{1,0:T(8,128)(2,1)} async-done(((bf16[72,512]{1,0:T(8,128)(2,1)}), bf16[1152,512]{1,0:T(8,128)(2,1)}) %all-gather.2.cloned.1.call-update) | async-done | bytes 1179664 | tf_op jit(solution)/shard_map/all_gather | solution.py:100
  257.3 2.5 fusion.24
  (106 shorter events, 24.5 us)
Async XLA Ops:
  7.2 9.5 %copy-start.3 = (bf16[4,1,8,128,128]{4,3,2,1,0:T(8,128)(2,1)S(1)}, bf16[4,1,8,128,128]{4,3,2,1,0:T(8,128)(2,1)}, u32[]{:S(2)}) copy-start(bf16[4,1,8,128,128]{4,3,2,1,0:T(8,128)(2,1)} %param.7) | copy-start | bytes 3145732
  7.2 148.5 %reduce-scatter.2.cloned.1.call-start = ((), (), s32[]{:S(2)}) async-start(), calls=%async_computation.1 | async-start | bytes 2506752 | tf_op jit(solution)/shard_map/reduce_scatter | solution.py:81
  9.2 11.0 %collective-permute-start.1 = (bf16[1,128,128]{1,2,0:T(8,128)(2,1)S(1)}, bf16[1,128,128]{1,2,0:T(8,128)(2,1)S(1)}, u32[]{:S(2)}, u32[]{:S(2)}) collective-permute-start(bf16[1,128,128]{1,2,0:T(8,128)(2,1)S(1)} %get-tuple-element.30), channel_id=1, source_target_pairs={{1,0},{3,2},{5,4},{7,6},{9,8},{11,10},{13,12},{15,14},{17,16},{19,... | collective-permute-start | bytes 98312 | tf_op jit(solution)/shard_map/ppermute | solution.py:18
  10.5 9.7 %collective-permute-start = (bf16[1,128,128]{1,2,0:T(8,128)(2,1)S(1)}, bf16[1,128,128]{1,2,0:T(8,128)(2,1)S(1)}, u32[]{:S(2)}, u32[]{:S(2)}) collective-permute-start(bf16[1,128,128]{1,2,0:T(8,128)(2,1)S(1)} %get-tuple-element.29), channel_id=1, source_target_pairs={{0,1},{2,3},{4,5},{6,7},{8,9},{10,11},{12,13},{14,15},{16,17},{18,... | collective-permute-start | bytes 98312 | tf_op jit(solution)/shard_map/ppermute | solution.py:16
  23.1 8.9 %copy-start.8 = (bf16[1,1,8,128,128]{4,3,2,1,0:T(8,128)(2,1)S(1)}, bf16[1,1,8,128,128]{4,3,2,1,0:T(8,128)(2,1)}, u32[]{:S(2)}) copy-start(bf16[1,1,8,128,128]{4,3,2,1,0:T(8,128)(2,1)} %get-tuple-element.18) | copy-start | bytes 786436
  25.6 7.5 %collective-permute-start.3 = (bf16[1,128,128]{2,1,0:T(8,128)(2,1)}, bf16[1,128,128]{2,1,0:T(8,128)(2,1)}, u32[]{:S(2)}, u32[]{:S(2)}) collective-permute-start(bf16[1,128,128]{2,1,0:T(8,128)(2,1)} %get-tuple-element.28), channel_id=1, source_target_pairs={{1,0},{3,2},{5,4},{7,6},{9,8},{11,10},{13,12},{15,14},{17,16},{19,... | collective-permute-start | bytes 98312 | tf_op jit(solution)/shard_map/ppermute | solution.py:18
  26.9 7.0 %collective-permute-start.2 = (bf16[1,128,128]{2,1,0:T(8,128)(2,1)}, bf16[1,128,128]{2,1,0:T(8,128)(2,1)S(1)}, u32[]{:S(2)}, u32[]{:S(2)}) collective-permute-start(bf16[1,128,128]{2,1,0:T(8,128)(2,1)} %get-tuple-element.27), channel_id=1, source_target_pairs={{0,1},{2,3},{4,5},{6,7},{8,9},{10,11},{12,13},{14,15},{16,17},{18,... | collective-permute-start | bytes 98312 | tf_op jit(solution)/shard_map/ppermute | solution.py:16
  41.2 10.0 %copy-start = (bf16[8,128,9,128]{1,0,3,2:T(8,128)(2,1)S(1)}, bf16[8,128,9,128]{1,0,3,2:T(8,128)(2,1)}, u32[]{:S(2)}) copy-start(bf16[8,128,9,128]{1,0,3,2:T(8,128)(2,1)} %copy.28) | copy-start | bytes 7077892
  41.2 10.0 %copy-start.7 = (bf16[1,1,8,128,128]{4,3,2,1,0:T(8,128)(2,1)S(1)}, bf16[1,1,8,128,128]{4,3,2,1,0:T(8,128)(2,1)}, u32[]{:S(2)}) copy-start(bf16[1,1,8,128,128]{4,3,2,1,0:T(8,128)(2,1)} %get-tuple-element.16) | copy-start | bytes 786436
  44.6 10.4 %collective-permute-start.5 = (bf16[1,128,128]{2,1,0:T(8,128)(2,1)}, bf16[1,128,128]{2,1,0:T(8,128)(2,1)}, u32[]{:S(2)}, u32[]{:S(2)}) collective-permute-start(bf16[1,128,128]{2,1,0:T(8,128)(2,1)} %get-tuple-element.26), channel_id=1, source_target_pairs={{1,0},{3,2},{5,4},{7,6},{9,8},{11,10},{13,12},{15,14},{17,16},{19,... | collective-permute-start | bytes 98312 | tf_op jit(solution)/shard_map/ppermute | solution.py:18
  45.9 9.1 %collective-permute-start.4 = (bf16[1,128,128]{2,1,0:T(8,128)(2,1)}, bf16[1,128,128]{2,1,0:T(8,128)(2,1)S(1)}, u32[]{:S(2)}, u32[]{:S(2)}) collective-permute-start(bf16[1,128,128]{2,1,0:T(8,128)(2,1)} %get-tuple-element.25), channel_id=1, source_target_pairs={{0,1},{2,3},{4,5},{6,7},{8,9},{10,11},{12,13},{14,15},{16,17},{18,... | collective-permute-start | bytes 98312 | tf_op jit(solution)/shard_map/ppermute | solution.py:16
  62.3 9.8 %copy-start.1 = (bf16[8,128,9,128]{1,0,3,2:T(8,128)(2,1)S(1)}, bf16[8,128,9,128]{1,0,3,2:T(8,128)(2,1)}, u32[]{:S(2)}) copy-start(bf16[8,128,9,128]{1,0,3,2:T(8,128)(2,1)} %copy.26) | copy-start | bytes 7077892
  62.3 9.8 %copy-start.6 = (bf16[1,1,8,128,128]{4,3,2,1,0:T(8,128)(2,1)S(1)}, bf16[1,1,8,128,128]{4,3,2,1,0:T(8,128)(2,1)}, u32[]{:S(2)}) copy-start(bf16[1,1,8,128,128]{4,3,2,1,0:T(8,128)(2,1)} %get-tuple-element.17) | copy-start | bytes 786436
  65.7 10.2 %collective-permute-start.7 = (bf16[1,128,128]{2,1,0:T(8,128)(2,1)}, bf16[1,128,128]{2,1,0:T(8,128)(2,1)}, u32[]{:S(2)}, u32[]{:S(2)}) collective-permute-start(bf16[1,128,128]{2,1,0:T(8,128)(2,1)} %get-tuple-element.24), channel_id=1, source_target_pairs={{1,0},{3,2},{5,4},{7,6},{9,8},{11,10},{13,12},{15,14},{17,16},{19,... | collective-permute-start | bytes 98312 | tf_op jit(solution)/shard_map/ppermute | solution.py:18
  67.0 8.9 %collective-permute-start.6 = (bf16[1,128,128]{2,1,0:T(8,128)(2,1)}, bf16[1,128,128]{2,1,0:T(8,128)(2,1)S(1)}, u32[]{:S(2)}, u32[]{:S(2)}) collective-permute-start(bf16[1,128,128]{2,1,0:T(8,128)(2,1)} %get-tuple-element.23), channel_id=1, source_target_pairs={{0,1},{2,3},{4,5},{6,7},{8,9},{10,11},{12,13},{14,15},{16,17},{18,... | collective-permute-start | bytes 98312 | tf_op jit(solution)/shard_map/ppermute | solution.py:16
  78.1 2.7 %copy-start.5 = (bf16[1,1,8,128,128]{4,3,2,1,0:T(8,128)(2,1)S(1)}, bf16[1,1,8,128,128]{4,3,2,1,0:T(8,128)(2,1)}, u32[]{:S(2)}) copy-start(bf16[1,1,8,128,128]{4,3,2,1,0:T(8,128)(2,1)} %get-tuple-element.15) | copy-start | bytes 786436
  91.1 0.7 copy-start.9
  91.1 11.6 %copy-start.2 = (bf16[2,72,1152]{2,1,0:T(8,128)(2,1)S(1)}, bf16[2,72,1152]{2,1,0:T(8,128)(2,1)}, u32[]{:S(2)}) copy-start(bf16[2,72,1152]{2,1,0:T(8,128)(2,1)} %param.12) | copy-start | bytes 995332
  91.1 66.2 %copy-start.4 = (bf16[2,128,128]{2,1,0:T(8,128)(2,1)S(1)}, bf16[2,128,128]{2,1,0:T(8,128)(2,1)}, u32[]{:S(2)}) copy-start(bf16[2,128,128]{2,1,0:T(8,128)(2,1)} %param.13) | copy-start | bytes 196612
  91.1 100.9 %all-reduce.11.cloned.1.call-start = ((), (), s32[]{:S(2)}) async-start(), calls=%async_computation.4 | async-start | bytes 1474560 | tf_op jit(solution)/shard_map/psum | solution.py:83
  157.3 59.2 %all-reduce.9.cloned.1.call-start = ((), (), s32[]{:S(2)}) async-start(), calls=%async_computation.3 | async-start | bytes 262144 | tf_op jit(solution)/shard_map/psum | solution.py:27
  158.0 99.3 %all-gather.2.cloned.1.call-start = ((), (), s32[]{:S(2)}) async-start(), calls=%async_computation.2 | async-start | bytes 1253376 | tf_op jit(solution)/shard_map/all_gather | solution.py:100
  194.9 62.4 %copy-start.10 = (bf16[1,72,1152]{2,1,0:T(8,128)(2,1)S(1)}, bf16[1,72,1152]{2,1,0:T(8,128)(2,1)}, u32[]{:S(2)}) copy-start(bf16[1,72,1152]{2,1,0:T(8,128)(2,1)} %get-tuple-element.7) | copy-start | bytes 497668
  194.9 62.4 %copy-start.11 = (bf16[1,72,1152]{2,1,0:T(8,128)(2,1)S(1)}, bf16[1,72,1152]{2,1,0:T(8,128)(2,1)}, u32[]{:S(2)}) copy-start(bf16[1,72,1152]{2,1,0:T(8,128)(2,1)} %get-tuple-element.8) | copy-start | bytes 497668
  194.9 62.4 %copy-start.12 = (bf16[1,72,1152]{2,1,0:T(8,128)(2,1)S(1)}, bf16[1,72,1152]{2,1,0:T(8,128)(2,1)}, u32[]{:S(2)}) copy-start(bf16[1,72,1152]{2,1,0:T(8,128)(2,1)} %get-tuple-element.9) | copy-start | bytes 497668
  194.9 62.4 %copy-start.13 = (bf16[1,72,1152]{2,1,0:T(8,128)(2,1)S(1)}, bf16[1,72,1152]{2,1,0:T(8,128)(2,1)}, u32[]{:S(2)}) copy-start(bf16[1,72,1152]{2,1,0:T(8,128)(2,1)} %get-tuple-element.10) | copy-start | bytes 497668
Sparse Core Ops, SparseCore 0:
  91.2 64.3 reduce-scatter.1
  159.0 32.9 all-reduce.10
  194.6 21.8 all-reduce.8
  218.9 38.3 all-gather.1
where the time goes:
time: 268 us; the launch traced here: 266 us
  waiting for transfers between devices  146 us (54%)
  local copies, waits for them, and re-layouts  37.2 us (14%)
  starting transfers between devices  25.7 us (10%)
  between operations  24.6 us (9%)
  matrix products  20.3 us (8%)
  other arithmetic  12.4 us (5%)
    reduce_scatter x1, waiting for transfers between devices, per_device(): lax.psum_scatter(grad_term, 'dp', scatter_dimension=0, tiled=True)  52.2 us
    all_gather x1, waiting for transfers between devices, per_device(): gathered_piece = lax.all_gather(grad_sum, 'dp', axis=0, tiled=True)  40.8 us
    psum x1, waiting for transfers between devices, per_device(): grad_sum = lax.psum(grad_rows.astype(jnp.bfloat16), 'own')  34 us
    ppermute x4, starting transfers between devices, extended(): lax.ppermute(tail, axis, [(i, (i + 1) % count) for i in range(ends)])  20.4 us
    psum x1, waiting for transfers between devices, from_root(): return lax.psum(block, axis)  18.3 us
    another operation x11, local copies, waits for them, and re-layouts, tap_matrix(): stacked = jnp.stack(pieces, axis=2)  17.2 us
    dot_general x4, matrix products, per_device(): lax.dot_general(tap_rows, kernel, (((1,), (1,)), ((), ())), preferred_ele...  10.5 us
    mul x8, local copies, waits for them, and re-layouts, per_device(): grad_block.reshape(9 * channels, channels) * grad_scale  8.66 us
  transfers between devices with their start and end apart: 12, of which 5 were waited for; matrix products, arithmetic and copies ran while one was open for 8% of the time, Pallas kernels for 0%

commit v1 on v0

--- a/solution.py
+++ b/solution.py
@@ -3,6 +3,27 @@
 import jax.numpy as jnp
 from jax import lax
 from jax.sharding import PartitionSpec as P
+from jax.lax import axis_index, axis_size, ppermute
+
+
+def edit_works(raw, dim_i):
+    raw = jnp.moveaxis(raw, 0, dim_i)
+    x_now = raw.shape
+    return raw.reshape(*x_now[:dim_i], x_now[dim_i] * x_now[dim_i + 1], *x_now[dim_i + 2 :])
+
+
+def wait_rates(work_x, comm_axis):
+    w_next = axis_size(comm_axis)
+    res, mat_out = (w_next, axis_index(comm_axis))
+    d_next, t1 = (work_x[None], 1)
+    while t1 < res:
+        newest = ppermute(d_next, comm_axis, tuple(((k, k ^ t1) for k in range(res))))
+        local_next = mat_out & t1 == 0
+        d_next = jnp.concatenate(
+            [jnp.where(local_next, d_next, newest), jnp.where(local_next, newest, d_next)]
+        )
+        t1 *= 2
+    return d_next
 
 
 def extended(cells, sides, width):
@@ -97,7 +118,11 @@
         right_panels.append(right_panel)
     left_stack = jnp.stack(left_panels, axis=0)
     right_stack = jnp.stack(right_panels, axis=0)
-    gathered_piece = lax.all_gather(grad_sum, "dp", axis=0, tiled=True)
+
+    def attach_trails_all(local_array, body, d_out):
+        return edit_works(wait_rates(local_array, body), d_out)
+
+    gathered_piece = attach_trails_all(grad_sum, body="dp", d_out=0)
     width_here = gathered_piece.shape[0]
     shaped_piece = gathered_piece.reshape(width_here, layer_count, channels)
     left_product = jnp.einsum(

time: 268 us -> 243 us (0.907)
  waiting for transfers between devices: 146 us -> 118 us
  starting transfers between devices: 25.7 us -> 29.4 us
    all_gather x1 -> x0, waiting for transfers between devices: 40.8 us -> none  [per_device(): gathered_piece = lax.all_gather(grad_sum, 'dp', axis=0, tiled=True)]
    ppermute x0 -> x4, waiting for transfers between devices: none -> 30.3 us  [wait_rates(): ppermute(d_next, comm_axis, tuple(((k, k ^ t1) for k in range(res))))]
    psum x1, waiting for transfers between devices: 18.3 us -> 0.02 us  [from_root(): return lax.psum(block, axis)]
    ppermute x0 -> x4, starting transfers between devices: none -> 5.5 us  [wait_rates(): ppermute(d_next, comm_axis, tuple(((k, k ^ t1) for k in range(res))))]
    select_n x0 -> x4, other arithmetic: none -> 3.08 us  [wait_rates(): jnp.where(local_next, d_next, newest)]
    unnamed x52 -> x56, local copies, waits for them, and re-layouts: 3.66 us -> 5.65 us
  transfers between devices with their start and end apart: 12 -> 15, of which waited for: 5 -> 7; matrix products, arithmetic and copies ran while one was open for 8% -> 8% of each run, Pallas kernels for 0% -> 0%
where the time goes in v1:
time: 243 us; the launch traced here: 242 us
  waiting for transfers between devices  118 us (49%)
  local copies, waits for them, and re-layouts  35.6 us (15%)
  starting transfers between devices  29.4 us (12%)
  between operations  25.2 us (10%)
  matrix products  18.1 us (7%)
  other arithmetic  15 us (6%)
    reduce_scatter x1, waiting for transfers between devices, per_device(): lax.psum_scatter(grad_term, 'dp', scatter_dimension=0, tiled=True)  52.4 us
    psum x1, waiting for transfers between devices, per_device(): grad_sum = lax.psum(grad_rows.astype(jnp.bfloat16), 'own')  34.8 us
    ppermute x4, waiting for transfers between devices, wait_rates(): ppermute(d_next, comm_axis, tuple(((k, k ^ t1) for k in range(res))))  30.3 us
    ppermute x4, starting transfers between devices, extended(): lax.ppermute(tail, axis, [(i, (i + 1) % count) for i in range(ends)])  18.7 us
    another operation x11, local copies, waits for them, and re-layouts, tap_matrix(): stacked = jnp.stack(pieces, axis=2)  17.3 us
    dot_general x4, matrix products, per_device(): lax.dot_general(tap_rows, kernel, (((1,), (1,)), ((), ())), preferred_ele...  10.5 us
    mul x8, local copies, waits for them, and re-layouts, per_device(): grad_block.reshape(9 * channels, channels) * grad_scale  6.53 us
    unnamed x56, local copies, waits for them, and re-layouts  5.65 us
  transfers between devices with their start and end apart: 15, of which 7 were waited for; matrix products, arithmetic and copies ran while one was open for 8% of the time, Pallas kernels for 0%

profile of v1, /device:TPU:0, one launch (start us, length us, event | category | flops | bytes accessed | tf_op | source)
XLA Modules:
  0.0 241.5 jit_solution(6085740306645142518)
XLA Ops:
  10.5 4.8 %collective-permute-start = (bf16[1,128,128]{1,2,0:T(8,128)(2,1)S(1)}, bf16[1,128,128]{1,2,0:T(8,128)(2,1)S(1)}, u32[]{:S(2)}, u32[]{:S(2)}) collective-permute-start(bf16[1,128,128]{1,2,0:T(8,128)(2,1)S(1)} %get-tuple-element.35), channel_id=1, source_target_pairs={{0,1},{2,3},{4,5},{6,7},{8,9},{10,11},{12,13},{14,15},{16,17},{18,... | collective-permute-start | bytes 98312 | tf_op jit(solution)/shard_map/ppermute | solution.py:37
  15.4 1.3 fusion.110
  21.5 1.6 copy.30
  23.1 1.8 fusion.13
  26.3 4.5 %collective-permute-start.2 = (bf16[1,128,128]{2,1,0:T(8,128)(2,1)S(1)}, bf16[1,128,128]{2,1,0:T(8,128)(2,1)S(1)}, u32[]{:S(2)}, u32[]{:S(2)}) collective-permute-start(bf16[1,128,128]{2,1,0:T(8,128)(2,1)S(1)} %get-tuple-element.33), channel_id=1, source_target_pairs={{0,1},{2,3},{4,5},{6,7},{8,9},{10,11},{12,13},{14,15},{16,17},{18,... | collective-permute-start | bytes 98312 | tf_op jit(solution)/shard_map/ppermute | solution.py:37
  34.0 2.7 %copy.28 = bf16[8,128,9,128]{1,0,3,2:T(8,128)(2,1)} copy(bf16[8,128,9,128]{3,1,0,2:T(8,128)(2,1)S(1)} %fusion.81) | data formatting | bytes 4718592 | tf_op jit(solution)/shard_map/stack | solution.py:62
  36.6 2.5 %copy.20 = bf16[8,128,9,128]{1,3,2,0:T(8,128)(2,1)} copy(bf16[8,128,9,128]{3,1,0,2:T(8,128)(2,1)S(1)} %fusion.81) | data formatting | bytes 4718592 | tf_op jit(solution)/shard_map/stack | solution.py:62
  39.1 2.7 %fusion.14 = bf16[8,128,128]{2,1,0:T(8,128)(2,1)S(1)} fusion(bf16[8,128,1152]{1,2,0:T(8,128)(2,1)} %bitcast.245, bf16[128,1152,1]{1,0,2:T(8,128)(2,1)} %reshape.131, bf16[4,1,8,128,128]{4,3,2,1,0:T(8,128)(2,1)} %param.7), kind=kOutput, calls=%fused_computation.24 | convolution fusion | flops 302383104 | bytes 3178496 | tf_op jit(solution)/shard_map/dot_general | solution.py:91
  43.2 4.7 %collective-permute-start.4 = (bf16[1,128,128]{2,1,0:T(8,128)(2,1)S(1)}, bf16[1,128,128]{2,1,0:T(8,128)(2,1)S(1)}, u32[]{:S(2)}, u32[]{:S(2)}) collective-permute-start(bf16[1,128,128]{2,1,0:T(8,128)(2,1)S(1)} %get-tuple-element.31), channel_id=1, source_target_pairs={{0,1},{2,3},{4,5},{6,7},{8,9},{10,11},{12,13},{14,15},{16,17},{18,... | collective-permute-start | bytes 98312 | tf_op jit(solution)/shard_map/ppermute | solution.py:37
  51.9 2.7 %copy.26 = bf16[8,128,9,128]{1,0,3,2:T(8,128)(2,1)} copy(bf16[8,128,9,128]{3,1,0,2:T(8,128)(2,1)S(1)} %fusion.71) | data formatting | bytes 4718592 | tf_op jit(solution)/shard_map/stack | solution.py:62
  54.6 2.5 %copy.22 = bf16[8,128,9,128]{1,3,2,0:T(8,128)(2,1)} copy(bf16[8,128,9,128]{3,1,0,2:T(8,128)(2,1)S(1)} %fusion.71) | data formatting | bytes 4718592 | tf_op jit(solution)/shard_map/stack | solution.py:62
  57.1 2.7 %fusion.15 = bf16[8,128,128]{2,1,0:T(8,128)(2,1)S(1)} fusion(bf16[8,128,1152]{1,2,0:T(8,128)(2,1)} %bitcast.246, bf16[128,1152,1]{1,0,2:T(8,128)(2,1)} %reshape.132, bf16[4,1,8,128,128]{4,3,2,1,0:T(8,128)(2,1)} %param.7), kind=kOutput, calls=%fused_computation.25 | convolution fusion | flops 302383104 | bytes 3178496 | tf_op jit(solution)/shard_map/dot_general | solution.py:91
  61.1 4.5 %collective-permute-start.6 = (bf16[1,128,128]{2,1,0:T(8,128)(2,1)S(1)}, bf16[1,128,128]{2,1,0:T(8,128)(2,1)S(1)}, u32[]{:S(2)}, u32[]{:S(2)}) collective-permute-start(bf16[1,128,128]{2,1,0:T(8,128)(2,1)S(1)} %get-tuple-element.29), channel_id=1, source_target_pairs={{0,1},{2,3},{4,5},{6,7},{8,9},{10,11},{12,13},{14,15},{16,17},{18,... | collective-permute-start | bytes 98312 | tf_op jit(solution)/shard_map/ppermute | solution.py:37
  69.6 2.7 %copy.24 = bf16[8,128,9,128]{1,0,3,2:T(8,128)(2,1)} copy(bf16[8,128,9,128]{3,1,0,2:T(8,128)(2,1)S(1)} %fusion.61) | data formatting | bytes 4718592 | tf_op jit(solution)/shard_map/stack | solution.py:62
  72.3 3.3 %fusion = f32[128,1152]{0,1:T(8,128)} fusion(bf16[1024,128]{1,0:T(8,128)(2,1)S(1)} %bitcast.248, bf16[144,8,8,128]{3,2,1,0:T(8,128)(2,1)} %bitcast.247), kind=kOutput, calls=%fused_computation.4 | convolution fusion | flops 302137344 | bytes 3211264 | tf_op jit(solution)/shard_map/dot_general | solution.py:86
  75.6 2.1 copy.25
  77.7 1.9 mul.59
  79.6 3.0 %pad_maximum_fusion = f32[1152,512]{1,0:T(8,128)} fusion(f32[1152,128]{1,0:T(8,128)S(1)} %mul.68, f32[1152,128]{1,0:T(8,128)} %mul.65, f32[1152,128]{1,0:T(8,128)} %mul.62, f32[1152,128]{1,0:T(8,128)} %mul.59), kind=kLoop, calls=%fused_computation.16 | loop fusion | flops 1769472 | bytes 4718592 | tf_op jit(solution)/shard_map/concatenate | solution.py:101
  95.6 52.4 %reduce-scatter.2.cloned.1.call-done = f32[72,512]{1,0:T(8,128)} async-done(((f32[1152,512]{1,0:T(8,128)}), f32[72,512]{1,0:T(8,128)}) %reduce-scatter.2.cloned.1.call-update) | async-done | bytes 147472 | tf_op jit(solution)/shard_map/reduce_scatter | solution.py:102
  148.0 1.6 convert_bitcast_fusion.2
  149.7 34.8 %all-reduce.11.cloned.1.call-done = (bf16[1,72,512]{2,1,0:T(8,128)(2,1)}, bf16[1,72,1152]{2,1,0:T(8,128)(2,1)}, bf16[1,72,1152]{2,1,0:T(8,128)(2,1)}, bf16[1,72,1152]{2,1,0:T(8,128)(2,1)}, bf16[1,72,1152]{2,1,0:T(8,128)(2,1)}) async-done(((bf16[1,72,512]{2,1,0:T(8,128)(2,1)}, bf16[1,72,1152]{2,1,0:T(8,128)(2,1)}, bf16[1,72,1152]{2,1,0:T(8,128)(2,1)}, bf16[1,72,1152]{2,1,0:T(8,128)(2,1)}, ...) | async-done | bytes 737296 | tf_op jit(solution)/shard_map/psum | solution.py:104
  184.4 1.5 collective-permute-done.8
  186.8 1.5 collective-permute-start.9
  188.4 4.4 %collective-permute-done.9 = bf16[2,72,512]{2,1,0:T(8,128)(2,1)S(1)} collective-permute-done((bf16[2,72,512]{2,1,0:T(8,128)(2,1)S(1)}, bf16[2,72,512]{2,1,0:T(8,128)(2,1)S(1)}, u32[]{:S(2)}, u32[]{:S(2)}) %collective-permute-start.9) | collective-permute-done | bytes 147488 | tf_op jit(solution)/shard_map/ppermute | solution.py:20
  192.9 1.6 collective-permute-start.10
  194.4 6.9 %collective-permute-done.10 = bf16[4,72,512]{2,1,0:T(8,128)(2,1)} collective-permute-done((bf16[4,72,512]{2,1,0:T(8,128)(2,1)S(1)}, bf16[4,72,512]{2,1,0:T(8,128)(2,1)}, u32[]{:S(2)}, u32[]{:S(2)}) %collective-permute-start.10) | collective-permute-done | bytes 294944 | tf_op jit(solution)/shard_map/ppermute | solution.py:20
  203.2 2.4 collective-permute-start.11
  205.6 1.5 dynamic-slice_select_fusion.7
  207.4 2.5 %copy.32 = bf16[8,128,9,128]{1,3,2,0:T(8,128)(2,1)} copy(bf16[8,128,9,128]{3,1,0,2:T(8,128)(2,1)S(1)} %fusion.61) | data formatting | bytes 4718592 | tf_op jit(solution)/shard_map/stack | solution.py:62
  209.9 3.2 %fusion.18 = bf16[1,8,128,128]{3,2,1,0:T(8,128)(2,1)} fusion(bf16[8,128,1152]{1,2,0:T(8,128)(2,1)} %bitcast.240, bf16[128,1152,1]{1,0,2:T(8,128)(2,1)S(1)} %reshape.133), kind=kOutput, calls=%fused_computation.30 | convolution fusion | flops 302120960 | bytes 2916352 | tf_op jit(solution)/shard_map/dot_general | solution.py:91
  213.2 17.5 %collective-permute-done.11 = bf16[8,72,512]{2,1,0:T(8,128)(2,1)} collective-permute-done((bf16[8,72,512]{2,1,0:T(8,128)(2,1)}, bf16[8,72,512]{2,1,0:T(8,128)(2,1)}, u32[]{:S(2)}, u32[]{:S(2)}) %collective-permute-start.11) | collective-permute-done | bytes 589856 | tf_op jit(solution)/shard_map/ppermute | solution.py:20
  233.0 2.0 fusion.23
  (124 shorter events, 30.4 us)
Async XLA Ops:
  7.2 9.5 %copy-start.3 = (bf16[4,1,8,128,128]{4,3,2,1,0:T(8,128)(2,1)S(1)}, bf16[4,1,8,128,128]{4,3,2,1,0:T(8,128)(2,1)}, u32[]{:S(2)}) copy-start(bf16[4,1,8,128,128]{4,3,2,1,0:T(8,128)(2,1)} %param.7) | copy-start | bytes 3145732
  7.2 140.9 %reduce-scatter.2.cloned.1.call-start = ((), (), s32[]{:S(2)}) async-start(), calls=%async_computation.1 | async-start | bytes 2506752 | tf_op jit(solution)/shard_map/reduce_scatter | solution.py:102
  9.2 11.0 %collective-permute-start.1 = (bf16[1,128,128]{1,2,0:T(8,128)(2,1)S(1)}, bf16[1,128,128]{1,2,0:T(8,128)(2,1)S(1)}, u32[]{:S(2)}, u32[]{:S(2)}) collective-permute-start(bf16[1,128,128]{1,2,0:T(8,128)(2,1)S(1)} %get-tuple-element.36), channel_id=1, source_target_pairs={{1,0},{3,2},{5,4},{7,6},{9,8},{11,10},{13,12},{15,14},{17,16},{19,... | collective-permute-start | bytes 98312 | tf_op jit(solution)/shard_map/ppermute | solution.py:39
  10.5 9.7 %collective-permute-start = (bf16[1,128,128]{1,2,0:T(8,128)(2,1)S(1)}, bf16[1,128,128]{1,2,0:T(8,128)(2,1)S(1)}, u32[]{:S(2)}, u32[]{:S(2)}) collective-permute-start(bf16[1,128,128]{1,2,0:T(8,128)(2,1)S(1)} %get-tuple-element.35), channel_id=1, source_target_pairs={{0,1},{2,3},{4,5},{6,7},{8,9},{10,11},{12,13},{14,15},{16,17},{18,... | collective-permute-start | bytes 98312 | tf_op jit(solution)/shard_map/ppermute | solution.py:37
  23.1 7.7 %copy-start.7 = (bf16[1,1,8,128,128]{4,3,2,1,0:T(8,128)(2,1)S(1)}, bf16[1,1,8,128,128]{4,3,2,1,0:T(8,128)(2,1)}, u32[]{:S(2)}) copy-start(bf16[1,1,8,128,128]{4,3,2,1,0:T(8,128)(2,1)} %get-tuple-element.20) | copy-start | bytes 786436
  25.0 6.9 %collective-permute-start.3 = (bf16[1,128,128]{2,1,0:T(8,128)(2,1)S(1)}, bf16[1,128,128]{2,1,0:T(8,128)(2,1)S(1)}, u32[]{:S(2)}, u32[]{:S(2)}) collective-permute-start(bf16[1,128,128]{2,1,0:T(8,128)(2,1)S(1)} %get-tuple-element.34), channel_id=1, source_target_pairs={{1,0},{3,2},{5,4},{7,6},{9,8},{11,10},{13,12},{15,14},{17,16},{19,... | collective-permute-start | bytes 98312 | tf_op jit(solution)/shard_map/ppermute | solution.py:39
  26.3 6.1 %collective-permute-start.2 = (bf16[1,128,128]{2,1,0:T(8,128)(2,1)S(1)}, bf16[1,128,128]{2,1,0:T(8,128)(2,1)S(1)}, u32[]{:S(2)}, u32[]{:S(2)}) collective-permute-start(bf16[1,128,128]{2,1,0:T(8,128)(2,1)S(1)} %get-tuple-element.33), channel_id=1, source_target_pairs={{0,1},{2,3},{4,5},{6,7},{8,9},{10,11},{12,13},{14,15},{16,17},{18,... | collective-permute-start | bytes 98312 | tf_op jit(solution)/shard_map/ppermute | solution.py:37
  31.9 0.6 copy-start.8
  39.1 8.8 %copy-start = (bf16[8,128,9,128]{1,0,3,2:T(8,128)(2,1)S(1)}, bf16[8,128,9,128]{1,0,3,2:T(8,128)(2,1)}, u32[]{:S(2)}) copy-start(bf16[8,128,9,128]{1,0,3,2:T(8,128)(2,1)} %copy.28) | copy-start | bytes 7077892
  39.1 8.8 %copy-start.6 = (bf16[1,1,8,128,128]{4,3,2,1,0:T(8,128)(2,1)S(1)}, bf16[1,1,8,128,128]{4,3,2,1,0:T(8,128)(2,1)}, u32[]{:S(2)}) copy-start(bf16[1,1,8,128,128]{4,3,2,1,0:T(8,128)(2,1)} %get-tuple-element.18) | copy-start | bytes 786436
  41.9 8.0 %collective-permute-start.5 = (bf16[1,128,128]{2,1,0:T(8,128)(2,1)S(1)}, bf16[1,128,128]{2,1,0:T(8,128)(2,1)S(1)}, u32[]{:S(2)}, u32[]{:S(2)}) collective-permute-start(bf16[1,128,128]{2,1,0:T(8,128)(2,1)S(1)} %get-tuple-element.32), channel_id=1, source_target_pairs={{1,0},{3,2},{5,4},{7,6},{9,8},{11,10},{13,12},{15,14},{17,16},{19,... | collective-permute-start | bytes 98312 | tf_op jit(solution)/shard_map/ppermute | solution.py:39
  43.2 6.7 %collective-permute-start.4 = (bf16[1,128,128]{2,1,0:T(8,128)(2,1)S(1)}, bf16[1,128,128]{2,1,0:T(8,128)(2,1)S(1)}, u32[]{:S(2)}, u32[]{:S(2)}) collective-permute-start(bf16[1,128,128]{2,1,0:T(8,128)(2,1)S(1)} %get-tuple-element.31), channel_id=1, source_target_pairs={{0,1},{2,3},{4,5},{6,7},{8,9},{10,11},{12,13},{14,15},{16,17},{18,... | collective-permute-start | bytes 98312 | tf_op jit(solution)/shard_map/ppermute | solution.py:37
  49.8 0.6 copy-start.9
  57.1 8.6 %copy-start.1 = (bf16[8,128,9,128]{1,0,3,2:T(8,128)(2,1)S(1)}, bf16[8,128,9,128]{1,0,3,2:T(8,128)(2,1)}, u32[]{:S(2)}) copy-start(bf16[8,128,9,128]{1,0,3,2:T(8,128)(2,1)} %copy.26) | copy-start | bytes 7077892
  57.1 8.6 %copy-start.5 = (bf16[1,1,8,128,128]{4,3,2,1,0:T(8,128)(2,1)S(1)}, bf16[1,1,8,128,128]{4,3,2,1,0:T(8,128)(2,1)}, u32[]{:S(2)}) copy-start(bf16[1,1,8,128,128]{4,3,2,1,0:T(8,128)(2,1)} %get-tuple-element.19) | copy-start | bytes 786436
  59.8 7.7 %collective-permute-start.7 = (bf16[1,128,128]{2,1,0:T(8,128)(2,1)S(1)}, bf16[1,128,128]{2,1,0:T(8,128)(2,1)S(1)}, u32[]{:S(2)}, u32[]{:S(2)}) collective-permute-start(bf16[1,128,128]{2,1,0:T(8,128)(2,1)S(1)} %get-tuple-element.30), channel_id=1, source_target_pairs={{1,0},{3,2},{5,4},{7,6},{9,8},{11,10},{13,12},{15,14},{17,16},{19,... | collective-permute-start | bytes 98312 | tf_op jit(solution)/shard_map/ppermute | solution.py:39
  61.1 6.5 %collective-permute-start.6 = (bf16[1,128,128]{2,1,0:T(8,128)(2,1)S(1)}, bf16[1,128,128]{2,1,0:T(8,128)(2,1)S(1)}, u32[]{:S(2)}, u32[]{:S(2)}) collective-permute-start(bf16[1,128,128]{2,1,0:T(8,128)(2,1)S(1)} %get-tuple-element.29), channel_id=1, source_target_pairs={{0,1},{2,3},{4,5},{6,7},{8,9},{10,11},{12,13},{14,15},{16,17},{18,... | collective-permute-start | bytes 98312 | tf_op jit(solution)/shard_map/ppermute | solution.py:37
  67.6 0.6 copy-start.10
  69.6 2.7 %copy-start.4 = (bf16[1,1,8,128,128]{4,3,2,1,0:T(8,128)(2,1)S(1)}, bf16[1,1,8,128,128]{4,3,2,1,0:T(8,128)(2,1)}, u32[]{:S(2)}) copy-start(bf16[1,1,8,128,128]{4,3,2,1,0:T(8,128)(2,1)} %get-tuple-element.17) | copy-start | bytes 786436
  82.6 0.7 copy-start.11
  82.6 12.1 %copy-start.2 = (bf16[2,72,1152]{2,1,0:T(8,128)(2,1)S(1)}, bf16[2,72,1152]{2,1,0:T(8,128)(2,1)}, u32[]{:S(2)}) copy-start(bf16[2,72,1152]{2,1,0:T(8,128)(2,1)} %param.12) | copy-start | bytes 995332
  82.6 101.8 %all-reduce.11.cloned.1.call-start = ((), (), s32[]{:S(2)}) async-start(), calls=%async_computation.3 | async-start | bytes 1474560 | tf_op jit(solution)/shard_map/psum | solution.py:104
  149.6 82.7 %all-reduce.9.cloned.1.call-start = ((), (), s32[]{:S(2)}) async-start(), calls=%async_computation.2 | async-start | bytes 262144 | tf_op jit(solution)/shard_map/psum | solution.py:48
  184.4 1.5 collective-permute-start.8
  186.8 6.0 %collective-permute-start.9 = (bf16[2,72,512]{2,1,0:T(8,128)(2,1)S(1)}, bf16[2,72,512]{2,1,0:T(8,128)(2,1)S(1)}, u32[]{:S(2)}, u32[]{:S(2)}) collective-permute-start(bf16[2,72,512]{2,1,0:T(8,128)(2,1)S(1)} %pad_maximum_fusion.12), channel_id=1, source_target_pairs={{0,4},{2,6},{4,0},{6,2},{8,12},{10,14},{12,8},{14,10},{16,20},{18,... | collective-permute-start | bytes 442376 | tf_op jit(solution)/shard_map/ppermute | solution.py:20
  192.9 8.4 %collective-permute-start.10 = (bf16[4,72,512]{2,1,0:T(8,128)(2,1)S(1)}, bf16[4,72,512]{2,1,0:T(8,128)(2,1)}, u32[]{:S(2)}, u32[]{:S(2)}) collective-permute-start(bf16[4,72,512]{2,1,0:T(8,128)(2,1)S(1)} %pad_maximum_fusion.3), channel_id=1, source_target_pairs={{0,8},{2,10},{4,12},{6,14},{8,0},{10,2},{12,4},{14,6},{16,24},{18,... | collective-permute-start | bytes 884744 | tf_op jit(solution)/shard_map/ppermute | solution.py:20
  203.2 27.5 %collective-permute-start.11 = (bf16[8,72,512]{2,1,0:T(8,128)(2,1)}, bf16[8,72,512]{2,1,0:T(8,128)(2,1)}, u32[]{:S(2)}, u32[]{:S(2)}) collective-permute-start(bf16[8,72,512]{2,1,0:T(8,128)(2,1)} %pad_maximum_fusion.2), channel_id=1, source_target_pairs={{0,16},{2,18},{4,20},{6,22},{8,24},{10,26},{12,28},{14,30},{16,0},... | collective-permute-start | bytes 1769480 | tf_op jit(solution)/shard_map/ppermute | solution.py:20
  231.8 0.9 copy-start.12
  231.8 1.0 copy-start.13
  231.8 1.1 copy-start.14
  231.8 1.1 copy-start.15
Sparse Core Ops, SparseCore 0:
  82.8 65.2 reduce-scatter.1
  151.4 32.9 all-reduce.10
  207.2 20.0 all-reduce.8
